TPU v7x, 32 devices: a whole 2x2x4 slice. The times are simulated.
32 devices in a mesh: fsdp: 8 (over z, y), ctx: 2 (over x), tp: 2 (over core).
Axes of the slice: x: 2, y: 2, z: 4, core: 2. Of those that a mesh axis runs over, the one named last changes fastest.
Arguments:
- tokens_in: bfloat16 [4096, 2048], P(('fsdp', 'ctx')), may hold values from -6 to 6
- doc_positions: int32 [4096], P(('fsdp', 'ctx')), may hold values from 0 to 383, as said below
- attn_gain: bfloat16 [2048], P('fsdp'), may hold values from 0.25 to 1.75
- query_weight: bfloat16 [2048, 2048], P('fsdp', 'tp'), may hold values from -1 to 1
- key_weight: bfloat16 [2048, 256], P('fsdp', 'tp'), may hold values from -1 to 1
- value_weight: bfloat16 [2048, 256], P('fsdp', 'tp'), may hold values from -0.125 to 0.125
- output_weight: bfloat16 [2048, 2048], P('fsdp', 'tp'), may hold values from -2 to 2
- mlp_gain: bfloat16 [2048], P('fsdp'), may hold values from 0.25 to 1.75
- gate_weight: bfloat16 [2048, 5632], P('fsdp', 'tp'), may hold values from -0.125 to 0.125
- up_weight: bfloat16 [2048, 5632], P('fsdp', 'tp'), may hold values from -0.125 to 0.125
- down_weight: bfloat16 [2048, 5632], P('fsdp', 'tp'), may hold values from -0.078125 to 0.078125
- cotangent: bfloat16 [4096, 2048], P(('fsdp', 'ctx')), may hold values from -6 to 6
Outputs:
- block_out: bfloat16 [4096, 2048], P(('fsdp', 'ctx'))
- grad_tokens: float32 [4096, 2048], P(('fsdp', 'ctx'))
- grad_attn_gain: float32 [2048], P('fsdp')
- grad_query: float32 [2048, 2048], P('fsdp', 'tp')
- grad_key: float32 [2048, 256], P('fsdp', 'tp')
- grad_value: float32 [2048, 256], P('fsdp', 'tp')
- grad_output: float32 [2048, 2048], P('fsdp', 'tp')
- grad_mlp_gain: float32 [2048], P('fsdp')
- grad_gate: float32 [2048, 5632], P('fsdp', 'tp')
- grad_up: float32 [2048, 5632], P('fsdp', 'tp')
- grad_down: float32 [2048, 5632], P('fsdp', 'tp')
Inputs may be any that keep to these rules, and one draw needn't show every extreme that they name: `doc_positions`: each sequence of 512 tokens is packed with documents and begins with a new one; a token's value is its offset within its document: 0 at a document's first token, rising by one along it. Documents hold 102 to 384 tokens, except that the last of a sequence may be cut short; some document holds exactly 384.
All inputs are finite; a program needn't handle non-finite values.
Results may differ from a plain program's by a relative error of at most 0.014.
The roundings to bfloat16 on the way count: a program that leaves them out, or rounds other values in their place, can miss the bound.
Values may be sent and summed in bfloat16 or wider, within the bound.
No kernel may reach another device: no remote copies, remote signals or barrier semaphores. Data moves between devices by JAX's collectives and lax.ppermute only.
A program may use at most 256 MiB of HBM per device.

v0:
```python
import jax
import jax.numpy as jnp
from jax import lax
from jax.sharding import PartitionSpec as P

HEADS = 32
KV_HEADS = 4
HEAD_DIM = 64
EPSILON = 1e-05
NEG_FILL = -1e30


def rotary_tables(positions):
    half_dim = HEAD_DIM // 2
    inverse = 1.0 / 10000.0 ** (jnp.arange(half_dim, dtype=jnp.float32) * (2.0 / HEAD_DIM))
    angles = positions.astype(jnp.float32)[:, None] * inverse[None, :]
    cosine_table = jnp.concatenate([jnp.cos(angles), jnp.cos(angles)], axis=-1)[:, None, :]
    sine_table = jnp.concatenate([jnp.sin(angles), jnp.sin(angles)], axis=-1)[:, None, :]
    return (cosine_table, sine_table)


def apply_rotary(values, cosine_table, sine_table):
    half_dim = values.shape[-1] // 2
    turned = jnp.concatenate([-values[..., half_dim:], values[..., :half_dim]], axis=-1)
    return values * cosine_table + turned * sine_table


def undo_rotary(gradient, cosine_table, sine_table):
    half_dim = gradient.shape[-1] // 2
    sined = gradient * sine_table
    return gradient * cosine_table + jnp.concatenate(
        [sined[..., half_dim:], -sined[..., :half_dim]], axis=-1
    )


def contract_last(left_array, right_array):
    return lax.dot_general(
        left_array, right_array, (((1,), (1,)), ((), ())), preferred_element_type=jnp.float32
    )


def contract_first(left_array, right_array):
    return lax.dot_general(
        left_array, right_array, (((0,), (0,)), ((), ())), preferred_element_type=jnp.float32
    )


def normed_fold(scaled, pieces):
    gain_float = pieces[0].astype(jnp.float32)
    normed = (scaled * gain_float[None, :]).astype(jnp.bfloat16)
    sums = tuple(
        (jnp.dot(normed, matrix, preferred_element_type=jnp.float32) for matrix in pieces[1:])
    )
    return sums + (normed, gain_float)


def row_fold(left_array, shard_piece):
    return jnp.dot(left_array, shard_piece, preferred_element_type=jnp.float32)


def column_fold(gradients_in, pieces):
    part_sum = contract_last(gradients_in[0], pieces[0])
    for grad_piece, weight_piece in zip(gradients_in[1:], pieces[1:]):
        part_sum = part_sum + contract_last(grad_piece, weight_piece)
    return part_sum


def column_map(left_array, shard_piece):
    return contract_last(left_array, shard_piece)


def tensor_total(partial_sum):
    return lax.psum(partial_sum, "tp")


def body(
    tokens_in,
    doc_positions,
    attn_gain,
    query_weight,
    key_weight,
    value_weight,
    output_weight,
    mlp_gain,
    gate_weight,
    up_weight,
    down_weight,
    cotangent,
):
    local_rows = tokens_in.shape[0]
    query_columns = query_weight.shape[1]
    key_columns = key_weight.shape[1]
    local_groups = key_columns // HEAD_DIM
    group_size = HEADS // KV_HEADS
    group_width = group_size * HEAD_DIM
    score_scale = HEAD_DIM ** (-0.5)
    tokens = tokens_in.astype(jnp.float32)
    rms_one = lax.rsqrt(jnp.mean(tokens * tokens, axis=-1, keepdims=True) + EPSILON)
    scaled_one = tokens * rms_one
    query_lin, key_lin, value_lin, normed_one, gain_one = normed_fold(
        scaled_one,
        (
            lax.all_gather(attn_gain, "fsdp", axis=0, tiled=True),
            lax.all_gather(query_weight, "fsdp", axis=0, tiled=True),
            lax.all_gather(key_weight, "fsdp", axis=0, tiled=True),
            lax.all_gather(value_weight, "fsdp", axis=0, tiled=True),
        ),
    )
    cosine_table, sine_table = rotary_tables(doc_positions)
    queries = (
        apply_rotary(query_lin.reshape(local_rows, -1, HEAD_DIM), cosine_table, sine_table)
        .astype(jnp.bfloat16)
        .reshape(local_rows, query_columns)
    )
    keys_low = (
        apply_rotary(key_lin.reshape(local_rows, -1, HEAD_DIM), cosine_table, sine_table)
        .astype(jnp.bfloat16)
        .reshape(local_rows, key_columns)
    )
    values_low = value_lin.astype(jnp.bfloat16)
    key_all, value_all = (
        lax.all_gather(keys_low, "ctx", axis=0, tiled=True),
        lax.all_gather(values_low, "ctx", axis=0, tiled=True),
    )
    key_count = key_all.shape[0]
    query_places = lax.axis_index("ctx") * local_rows + jnp.arange(local_rows, dtype=jnp.int32)
    key_places = jnp.arange(key_count, dtype=jnp.int32)
    allowed = (key_places[None, :] <= query_places[:, None]) & (
        key_places[None, :] >= (query_places - doc_positions)[:, None]
    )

    def head_scores(query_group, key_head):
        raw_scores = (
            jnp.einsum("ngd,kd->gnk", query_group, key_head, preferred_element_type=jnp.float32)
            * score_scale
        )
        return jnp.where(allowed[None], raw_scores, NEG_FILL)

    attended_parts = []
    lse_parts = []
    for group_index in range(local_groups):
        query_group = queries[
            :, group_index * group_width : (group_index + 1) * group_width
        ].reshape(local_rows, group_size, HEAD_DIM)
        key_head = key_all[:, group_index * HEAD_DIM : (group_index + 1) * HEAD_DIM]
        value_head = value_all[:, group_index * HEAD_DIM : (group_index + 1) * HEAD_DIM]
        scores = head_scores(query_group, key_head)
        largest = jnp.max(scores, axis=-1, keepdims=True)
        exponent = jnp.exp(scores - largest)
        totals = jnp.sum(exponent, axis=-1, keepdims=True)
        probs_low = (exponent / totals).astype(jnp.bfloat16)
        attended_parts.append(
            jnp.einsum(
                "gnk,kd->ngd", probs_low, value_head, preferred_element_type=jnp.float32
            ).reshape(local_rows, group_width)
        )
        lse_parts.append(largest + jnp.log(totals))
    attended_low = jnp.concatenate(attended_parts, axis=1).astype(jnp.bfloat16)
    attn_branch = tensor_total(
        column_map(attended_low, lax.all_gather(output_weight, "fsdp", axis=0, tiled=True))
    )
    residual = tokens + attn_branch
    rms_two = lax.rsqrt(jnp.mean(residual * residual, axis=-1, keepdims=True) + EPSILON)
    scaled_two = residual * rms_two
    gate_lin, up_lin, normed_two, gain_two = normed_fold(
        scaled_two,
        (
            lax.all_gather(mlp_gain, "fsdp", axis=0, tiled=True),
            lax.all_gather(gate_weight, "fsdp", axis=0, tiled=True),
            lax.all_gather(up_weight, "fsdp", axis=0, tiled=True),
        ),
    )
    silu_value = gate_lin / (1.0 + jnp.exp(-gate_lin))
    act_low = (silu_value * up_lin).astype(jnp.bfloat16)
    mlp_branch = tensor_total(
        column_map(act_low, lax.all_gather(down_weight, "fsdp", axis=0, tiled=True))
    )
    block_out = (residual + mlp_branch).astype(jnp.bfloat16)
    grad_out = cotangent.astype(jnp.float32)
    grad_act = row_fold(cotangent, lax.all_gather(down_weight, "fsdp", axis=0, tiled=True))
    sigmoid = 1.0 / (1.0 + jnp.exp(-gate_lin))
    grad_gate_lin = (grad_act * up_lin * sigmoid * (1.0 + gate_lin * (1.0 - sigmoid))).astype(
        jnp.bfloat16
    )
    grad_up_lin = (grad_act * silu_value).astype(jnp.bfloat16)
    grad_normed_two = tensor_total(
        column_fold(
            (grad_gate_lin, grad_up_lin),
            (
                lax.all_gather(gate_weight, "fsdp", axis=0, tiled=True),
                lax.all_gather(up_weight, "fsdp", axis=0, tiled=True),
            ),
        )
    )
    scaled_grad_two = grad_normed_two * gain_two[None, :]
    grad_residual = (
        grad_out
        + rms_two * scaled_grad_two
        - residual
        * (rms_two * rms_two * rms_two)
        * jnp.mean(scaled_grad_two * residual, axis=-1, keepdims=True)
    )
    grad_attn_low = grad_residual.astype(jnp.bfloat16)
    grad_attended = row_fold(
        grad_attn_low, lax.all_gather(output_weight, "fsdp", axis=0, tiled=True)
    ).astype(jnp.bfloat16)
    query_grads = []
    key_grads = []
    value_grads = []
    for group_index in range(local_groups):
        query_group = queries[
            :, group_index * group_width : (group_index + 1) * group_width
        ].reshape(local_rows, group_size, HEAD_DIM)
        key_head = key_all[:, group_index * HEAD_DIM : (group_index + 1) * HEAD_DIM]
        value_head = value_all[:, group_index * HEAD_DIM : (group_index + 1) * HEAD_DIM]
        probabilities = jnp.exp(head_scores(query_group, key_head) - lse_parts[group_index])
        probs_low = probabilities.astype(jnp.bfloat16)
        grad_group = grad_attended[
            :, group_index * group_width : (group_index + 1) * group_width
        ].reshape(local_rows, group_size, HEAD_DIM)
        grad_probs = jnp.einsum(
            "ngd,kd->gnk", grad_group, value_head, preferred_element_type=jnp.float32
        )
        row_dot = jnp.sum(probabilities * grad_probs, axis=-1, keepdims=True)
        grad_scores = (probabilities * (grad_probs - row_dot)).astype(jnp.bfloat16)
        query_grads.append(
            jnp.einsum("gnk,kd->ngd", grad_scores, key_head, preferred_element_type=jnp.float32)
            * score_scale
        )
        key_grads.append(
            jnp.einsum("gnk,ngd->kd", grad_scores, query_group, preferred_element_type=jnp.float32)
            * score_scale
        )
        value_grads.append(
            jnp.einsum("gnk,ngd->kd", probs_low, grad_group, preferred_element_type=jnp.float32)
        )
    key_grad_local, value_grad_local = (
        lax.psum_scatter(
            jnp.concatenate(key_grads, axis=1), "ctx", scatter_dimension=0, tiled=True
        ),
        lax.psum_scatter(
            jnp.concatenate(value_grads, axis=1), "ctx", scatter_dimension=0, tiled=True
        ),
    )
    grad_q_lin = (
        undo_rotary(jnp.concatenate(query_grads, axis=1), cosine_table, sine_table)
        .astype(jnp.bfloat16)
        .reshape(local_rows, query_columns)
    )
    grad_k_lin = (
        undo_rotary(key_grad_local.reshape(local_rows, -1, HEAD_DIM), cosine_table, sine_table)
        .astype(jnp.bfloat16)
        .reshape(local_rows, key_columns)
    )
    grad_v_lin = value_grad_local.astype(jnp.bfloat16)
    grad_normed_one = tensor_total(
        column_fold(
            (grad_q_lin, grad_k_lin, grad_v_lin),
            (
                lax.all_gather(query_weight, "fsdp", axis=0, tiled=True),
                lax.all_gather(key_weight, "fsdp", axis=0, tiled=True),
                lax.all_gather(value_weight, "fsdp", axis=0, tiled=True),
            ),
        )
    )
    scaled_grad_one = grad_normed_one * gain_one[None, :]
    grad_tokens = (
        grad_residual
        + rms_one * scaled_grad_one
        - tokens
        * (rms_one * rms_one * rms_one)
        * jnp.mean(scaled_grad_one * tokens, axis=-1, keepdims=True)
    )
    owned = lax.psum_scatter(
        (
            jnp.sum(grad_normed_one * scaled_one, axis=0),
            contract_first(normed_one, grad_q_lin),
            contract_first(normed_one, grad_k_lin),
            contract_first(normed_one, grad_v_lin),
            contract_first(grad_attn_low, attended_low),
            jnp.sum(grad_normed_two * scaled_two, axis=0),
            contract_first(normed_two, grad_gate_lin),
            contract_first(normed_two, grad_up_lin),
            contract_first(cotangent, act_low),
        ),
        "fsdp",
        scatter_dimension=0,
        tiled=True,
    )
    (
        gain_one_grad,
        query_grad,
        key_grad,
        value_grad,
        output_grad,
        gain_two_grad,
        gate_grad,
        up_grad,
        down_grad,
    ) = owned
    summed = lax.psum(
        (
            gain_one_grad,
            query_grad,
            key_grad,
            value_grad,
            output_grad,
            gain_two_grad,
            gate_grad,
            up_grad,
            down_grad,
        ),
        "ctx",
    )
    return (
        block_out,
        grad_tokens,
        summed[0],
        summed[1],
        summed[2],
        summed[3],
        summed[4],
        summed[5],
        summed[6],
        summed[7],
        summed[8],
    )


def solution(mesh):
    return jax.shard_map(
        body,
        mesh=mesh,
        in_specs=(
            P(("fsdp", "ctx"), None),
            P(("fsdp", "ctx")),
            P("fsdp"),
            P("fsdp", "tp"),
            P("fsdp", "tp"),
            P("fsdp", "tp"),
            P("fsdp", "tp"),
            P("fsdp"),
            P("fsdp", "tp"),
            P("fsdp", "tp"),
            P("fsdp", "tp"),
            P(("fsdp", "ctx"), None),
        ),
        out_specs=(
            P(("fsdp", "ctx"), None),
            P(("fsdp", "ctx"), None),
            P("fsdp"),
            P("fsdp", "tp"),
            P("fsdp", "tp"),
            P("fsdp", "tp"),
            P("fsdp", "tp"),
            P("fsdp"),
            P("fsdp", "tp"),
            P("fsdp", "tp"),
            P("fsdp", "tp"),
        ),
        check_vma=False,
    )
```

profile of v0, /device:TPU:0, one launch (start us, length us, event | category | flops | bytes accessed | tf_op | source)
XLA Modules:
  0.0 2660.1 jit_solution(7111655742602666391)
XLA Ops:
  9.4 22.6 all-gather
  35.1 33.7 %all_gather.43 = bf16[2048,128]{1,0:T(8,128)(2,1)S(1)} all-gather(bf16[256,128]{1,0:T(8,128)(2,1)S(1)} %copy-done.46), channel_id=1, replica_groups=mesh['fsdp'=8,'ctx'=2,'tp'=2] {'fsdp'}, dimensions={0}, use_global_device_ids=true | all-gather | bytes 589824 | tf_op jit(solution)/shard_map/all_gather | solution.py:105
  75.1 32.7 %all_gather.41 = bf16[2048,128]{1,0:T(8,128)(2,1)S(1)} all-gather(bf16[256,128]{1,0:T(8,128)(2,1)S(1)} %copy-done.47), channel_id=1, replica_groups=mesh['fsdp'=8,'ctx'=2,'tp'=2] {'fsdp'}, dimensions={0}, use_global_device_ids=true | all-gather | bytes 589824 | tf_op jit(solution)/shard_map/all_gather | solution.py:106
  131.4 39.2 %all-gather.10.cloned.1.call-done = bf16[2048,1024]{1,0:T(8,128)(2,1)} async-done(((bf16[256,1024]{1,0:T(8,128)(2,1)}), bf16[2048,1024]{1,0:T(8,128)(2,1)}) %all-gather.10.cloned.1.call-update) | async-done | bytes 4194320 | tf_op jit(solution)/shard_map/all_gather | solution.py:160
  177.3 18.3 all-gather.1
  200.0 162.1 %all-gather.14.cloned.1.call-done = bf16[2048,2816]{1,0:T(8,128)(2,1)} async-done(((bf16[256,2816]{1,0:T(8,128)(2,1)}), bf16[2048,2816]{1,0:T(8,128)(2,1)}) %all-gather.14.cloned.1.call-update) | async-done | bytes 11534352 | tf_op jit(solution)/shard_map/all_gather | solution.py:170
  371.4 154.2 %all-gather.12.cloned.1.call-done = bf16[2048,2816]{1,0:T(8,128)(2,1)} async-done(((bf16[256,2816]{1,0:T(8,128)(2,1)}), bf16[2048,2816]{1,0:T(8,128)(2,1)}) %all-gather.12.cloned.1.call-update) | async-done | bytes 11534352 | tf_op jit(solution)/shard_map/all_gather | solution.py:169
  534.9 154.2 %all-gather.16.cloned.1.call-done = bf16[2048,2816]{1,0:T(8,128)(2,1)} async-done(((bf16[256,2816]{1,0:T(8,128)(2,1)}), bf16[2048,2816]{1,0:T(8,128)(2,1)}) %all-gather.16.cloned.1.call-update) | async-done | bytes 11534352 | tf_op jit(solution)/shard_map/all_gather | solution.py:176
  689.2 11.1 multiply_convert_fusion
  718.9 16.9 all-reduce.13.cloned.1.call-done
  777.8 11.7 reduce-scatter.10.cloned.1.call-done
  809.2 12.6 convolution_bitcast_fusion
  821.8 12.6 fusion.79
  834.7 12.6 fusion.78
  847.5 9.4 fusion.75
  861.1 63.5 %reduce-scatter.16.cloned.1.call-done = f32[256,128]{1,0:T(8,128)} async-done(((f32[2048,128]{1,0:T(8,128)}), f32[256,128]{1,0:T(8,128)}) %reduce-scatter.16.cloned.1.call-update) | async-done | bytes 131088 | tf_op jit(solution)/shard_map/reduce_scatter | solution.py:274
  924.6 149.9 %reduce-scatter.20.cloned.1.call-done = f32[256,1024]{1,0:T(8,128)} async-done(((f32[2048,1024]{1,0:T(8,128)}), f32[256,1024]{1,0:T(8,128)}) %reduce-scatter.20.cloned.1.call-update) | async-done | bytes 1048592 | tf_op jit(solution)/shard_map/reduce_scatter | solution.py:274
  1074.5 150.2 %reduce-scatter.14.cloned.1.call-done = f32[256,1024]{1,0:T(8,128)} async-done(((f32[2048,1024]{1,0:T(8,128)}), f32[256,1024]{1,0:T(8,128)}) %reduce-scatter.14.cloned.1.call-update) | async-done | bytes 1048592 | tf_op jit(solution)/shard_map/reduce_scatter | solution.py:274
  1224.8 376.5 %reduce-scatter.26.cloned.1.call-done = f32[256,2816]{0,1:T(8,128)} async-done(((f32[2048,2816]{0,1:T(8,128)}), f32[256,2816]{0,1:T(8,128)}) %reduce-scatter.26.cloned.1.call-update) | async-done | bytes 2883600 | tf_op jit(solution)/shard_map/reduce_scatter | solution.py:274
  1601.3 375.6 %reduce-scatter.24.cloned.1.call-done = f32[256,2816]{1,0:T(8,128)} async-done(((f32[2048,2816]{1,0:T(8,128)}), f32[256,2816]{1,0:T(8,128)}) %reduce-scatter.24.cloned.1.call-update) | async-done | bytes 2883600 | tf_op jit(solution)/shard_map/reduce_scatter | solution.py:274
  1976.9 375.6 %reduce-scatter.22.cloned.1.call-done = f32[256,2816]{1,0:T(8,128)} async-done(((f32[2048,2816]{1,0:T(8,128)}), f32[256,2816]{1,0:T(8,128)}) %reduce-scatter.22.cloned.1.call-update) | async-done | bytes 2883600 | tf_op jit(solution)/shard_map/reduce_scatter | solution.py:274
  2354.5 28.6 %all-reduce.15.cloned.1.call-done = (f32[256,2048]{1,0:T(8,128)}, f32[256,2048]{1,0:T(8,128)}) async-done(((f32[256,2048]{1,0:T(8,128)}, f32[256,2048]{1,0:T(8,128)}), (f32[256,2048]{1,0:T(8,128)}, f32[256,2048]{1,0:T(8,128)})) %all-reduce.15.cloned.1.call-update) | async-done | bytes 4194320 | tf_op jit(solution)/shard_map/psum | solution.py:73
  2385.3 37.3 %all-reduce.2 = (f32[2048]{0:T(1024)S(1)}, f32[2048]{0:T(1024)S(1)}) all-reduce(f32[2048]{0:T(1024)S(1)} %get-tuple-element.46, f32[2048]{0:T(1024)S(1)} %copy-done.52), channel_id=4, replica_groups=mesh['fsdp'=8,'ctx'=2,'tp'=2] {'fsdp'}, use_global_device_ids=true, to_apply=%region_17.18.clone | all-reduce | flops 4096 | bytes 32768
  2433.6 208.2 %all-reduce.17.cloned.1.call-done = (f32[256,1024]{1,0:T(8,128)}, f32[256,128]{1,0:T(8,128)}, f32[256,128]{1,0:T(8,128)}, f32[256,1024]{1,0:T(8,128)}, f32[256,2...) async-done(((f32[256,1024]{1,0:T(8,128)}, f32[256,128]{1,0:T(8,128)}, f32[256,128]{1,0:T(8,128)}, f32[256,1024]{1,0:T(8,128)}, f32[256,2816]{1,0:T(8,128)}, ...) | async-done | bytes 11010064 | tf_op jit(solution)/shard_map/psum | solution.py:301
  (259 shorter events, 174.5 us)
Async XLA Ops:
  7.2 61.7 %copy-start.5 = (bf16[256,2048]{1,0:T(8,128)(2,1)S(1)}, bf16[256,2048]{1,0:T(8,128)(2,1)}, u32[]{:S(2)}) copy-start(bf16[256,2048]{1,0:T(8,128)(2,1)} %param.12) | copy-start | bytes 3145732
  7.2 106.9 %all-gather.8.cloned.1.call-start = ((), (), s32[]{:S(2)}) async-start(), calls=%async_computation.9 | async-start | bytes 4718592 | tf_op jit(solution)/shard_map/all_gather | solution.py:104
  7.9 162.7 %all-gather.10.cloned.1.call-start = ((), (), s32[]{:S(2)}) async-start(), calls=%async_computation.10 | async-start | bytes 4718592 | tf_op jit(solution)/shard_map/all_gather | solution.py:160
  8.7 187.0 %all-reduce.11.cloned.1.call-start = ((), (), s32[]{:S(2)}) async-start(), calls=%async_computation.11 | async-start | bytes 4194304 | tf_op jit(solution)/shard_map/psum | solution.py:73
  35.1 79.0 %copy-start.48 = (f32[256]{0:T(256)}, f32[256]{0:T(256)S(1)}, u32[]{:S(2)}) copy-start(f32[256]{0:T(256)S(1)} %get-tuple-element.83) | copy-start | bytes 3076
  130.6 40.1 %copy-start.37 = (bf16[64,8,256]{2,0,1:T(8,128)(2,1)}, bf16[64,8,256]{2,0,1:T(8,128)(2,1)S(1)}, u32[]{:S(2)}) copy-start(bf16[64,8,256]{2,0,1:T(8,128)(2,1)S(1)} %fusion.29) | copy-start | bytes 786436
  131.4 44.1 %copy-start.38 = (bf16[64,8,256]{2,0,1:T(8,128)(2,1)}, bf16[64,8,256]{2,0,1:T(8,128)(2,1)S(1)}, u32[]{:S(2)}) copy-start(bf16[64,8,256]{2,0,1:T(8,128)(2,1)S(1)} %fusion.30) | copy-start | bytes 786436
  175.5 186.5 %all-gather.14.cloned.1.call-start = ((), (), s32[]{:S(2)}) async-start(), calls=%async_computation.13 | async-start | bytes 12976128 | tf_op jit(solution)/shard_map/all_gather | solution.py:170
  176.1 349.5 %all-gather.12.cloned.1.call-start = ((), (), s32[]{:S(2)}) async-start(), calls=%async_computation.12 | async-start | bytes 12976128 | tf_op jit(solution)/shard_map/all_gather | solution.py:169
  176.7 512.5 %all-gather.16.cloned.1.call-start = ((), (), s32[]{:S(2)}) async-start(), calls=%async_computation.14 | async-start | bytes 12976128 | tf_op jit(solution)/shard_map/all_gather | solution.py:176
  177.3 558.6 %all-reduce.13.cloned.1.call-start = ((), (), s32[]{:S(2)}) async-start(), calls=%async_computation.15 | async-start | bytes 4194304 | tf_op jit(solution)/shard_map/psum | solution.py:73
  716.2 58.7 %reduce-scatter.12.cloned.1.call-start = ((), (), s32[]{:S(2)}) async-start(), calls=%async_computation.17 | async-start | bytes 393216 | tf_op jit(solution)/shard_map/reduce_scatter | solution.py:241
  761.8 27.7 %reduce-scatter.10.cloned.1.call-start = ((), (), s32[]{:S(2)}) async-start(), calls=%async_computation.16 | async-start | bytes 393216 | tf_op jit(solution)/shard_map/reduce_scatter | solution.py:238
  771.8 89.3 %reduce-scatter.18.cloned.1.call-start = ((), (), s32[]{:S(2)}) async-start(), calls=%async_computation.20 | async-start | bytes 1179648 | tf_op jit(solution)/shard_map/reduce_scatter | solution.py:274
  777.4 147.2 %reduce-scatter.16.cloned.1.call-start = ((), (), s32[]{:S(2)}) async-start(), calls=%async_computation.19 | async-start | bytes 1179648 | tf_op jit(solution)/shard_map/reduce_scatter | solution.py:274
  793.0 281.6 %reduce-scatter.20.cloned.1.call-start = ((), (), s32[]{:S(2)}) async-start(), calls=%async_computation.21 | async-start | bytes 9437184 | tf_op jit(solution)/shard_map/reduce_scatter | solution.py:274
  799.3 425.4 %reduce-scatter.14.cloned.1.call-start = ((), (), s32[]{:S(2)}) async-start(), calls=%async_computation.18 | async-start | bytes 9437184 | tf_op jit(solution)/shard_map/reduce_scatter | solution.py:274
  809.1 792.1 %reduce-scatter.26.cloned.1.call-start = ((), (), s32[]{:S(2)}) async-start(), calls=%async_computation.24 | async-start | bytes 25952256 | tf_op jit(solution)/shard_map/reduce_scatter | solution.py:274
  821.8 1155.1 %reduce-scatter.24.cloned.1.call-start = ((), (), s32[]{:S(2)}) async-start(), calls=%async_computation.23 | async-start | bytes 25952256 | tf_op jit(solution)/shard_map/reduce_scatter | solution.py:274
  834.5 1518.1 %reduce-scatter.22.cloned.1.call-start = ((), (), s32[]{:S(2)}) async-start(), calls=%async_computation.22 | async-start | bytes 25952256 | tf_op jit(solution)/shard_map/reduce_scatter | solution.py:274
  847.4 1535.7 %all-reduce.15.cloned.1.call-start = ((), (), s32[]{:S(2)}) async-start(), calls=%async_computation.25 | async-start | bytes 8388608 | tf_op jit(solution)/shard_map/psum | solution.py:73
  861.0 1780.8 %all-reduce.17.cloned.1.call-start = ((), (), s32[]{:S(2)}) async-start(), calls=%async_computation.26 | async-start | bytes 22020096 | tf_op jit(solution)/shard_map/psum | solution.py:301
  2352.6 32.8 %copy-start.52 = (f32[2048]{0:T(1024)S(1)}, f32[2048]{0:T(1024)}, u32[]{:S(2)}) copy-start(f32[2048]{0:T(1024)} %get-tuple-element.44) | copy-start | bytes 24580
  2352.6 75.9 %copy-start.56 = (f32[256]{0:T(256)S(1)}, f32[256]{0:T(256)}, u32[]{:S(2)}) copy-start(f32[256]{0:T(256)} %get-tuple-element.82) | copy-start | bytes 3076
  (56 other events, 195.6 us)
Sparse Core Ops, SparseCore 0:
  10.1 86.2 all-gather.7
  98.6 72.0 all-gather.9
  175.6 19.8 all-reduce.10
  197.5 164.4 all-gather.13
  364.1 161.4 all-gather.11
  527.7 161.4 all-gather.15
  716.3 19.4 all-reduce.12
  761.9 12.9 reduce-scatter.11
  777.7 11.7 reduce-scatter.9
  793.3 64.1 reduce-scatter.17
  861.5 63.0 reduce-scatter.15
  928.1 146.3 reduce-scatter.19
  1078.2 146.5 reduce-scatter.13
  1228.5 372.7 reduce-scatter.25
  1605.0 371.8 reduce-scatter.23
  1980.6 371.8 reduce-scatter.21
  2355.5 27.5 all-reduce.14
  2386.0 255.8 all-reduce.16
where the time goes:
time: 2670 us; the launch traced here: 2660 us
  waiting for transfers between devices  2270 us (85%)
  blocking collectives  160 us (6%)
  matrix products  144 us (5%)
  other arithmetic  35.2 us (1%)
  local copies, waits for them, and re-layouts  30.6 us (1%)
    reduce_scatter x7, waiting for transfers between devices, body(): lax.psum_scatter((jnp.sum(grad_normed_one * scaled_one, axis=0), contract...  1490 us
    psum x1, waiting for transfers between devices, body(): lax.psum((gain_one_grad, query_grad, key_grad, value_grad, output_grad, g...  208 us
    all_gather x1, waiting for transfers between devices, body(): lax.all_gather(up_weight, 'fsdp', axis=0, tiled=True)  162 us
    all_gather x1, waiting for transfers between devices, body(): lax.all_gather(down_weight, 'fsdp', axis=0, tiled=True)  154 us
    all_gather x1, waiting for transfers between devices, body(): lax.all_gather(gate_weight, 'fsdp', axis=0, tiled=True)  154 us
  transfers between devices with their start and end apart: 18, of which 15 were waited for; matrix products, arithmetic and copies ran while one was open for 5% of the time, Pallas kernels for 0%

commit v1 on v0

--- a/solution.py
+++ b/solution.py
@@ -173,7 +173,13 @@
     silu_value = gate_lin / (1.0 + jnp.exp(-gate_lin))
     act_low = (silu_value * up_lin).astype(jnp.bfloat16)
     mlp_branch = tensor_total(
-        column_map(act_low, lax.all_gather(down_weight, "fsdp", axis=0, tiled=True))
+        column_map(
+            act_low,
+            jnp.concatenate(
+                lax.all_to_all(jnp.stack([down_weight] * lax.axis_size("fsdp")), "fsdp", 0, 0),
+                axis=0,
+            ),
+        )
     )
     block_out = (residual + mlp_branch).astype(jnp.bfloat16)
     grad_out = cotangent.astype(jnp.float32)

time: 2670 us -> 2810 us (1.052)
  blocking collectives: 160 us -> 540 us
  waiting for transfers between devices: 2270 us -> 2030 us
    all_to_all x0 -> x1, blocking collectives: none -> 379 us  [body(): lax.all_to_all(jnp.stack([down_weight] * lax.axis_size('fsdp')), 'fsdp',...]
    reduce_scatter x7, waiting for transfers between devices: 1490 us -> 1250 us  [body(): lax.psum_scatter((jnp.sum(grad_normed_one * scaled_one, axis=0), contract...]
  transfers between devices with their start and end apart: 18 -> 18, of which waited for: 15 -> 13; matrix products, arithmetic and copies ran while one was open for 5% -> 5% of each run, Pallas kernels for 0% -> 0%
where the time goes in v1:
time: 2810 us; the launch traced here: 2800 us
  waiting for transfers between devices  2030 us (72%)
  blocking collectives  540 us (19%)
  matrix products  141 us (5%)
  local copies, waits for them, and re-layouts  36.2 us (1%)
  other arithmetic  35.2 us (1%)
    reduce_scatter x7, waiting for transfers between devices, body(): lax.psum_scatter((jnp.sum(grad_normed_one * scaled_one, axis=0), contract...  1250 us
    all_to_all x1, blocking collectives, body(): lax.all_to_all(jnp.stack([down_weight] * lax.axis_size('fsdp')), 'fsdp',...  379 us
    psum x1, waiting for transfers between devices, body(): lax.psum((gain_one_grad, query_grad, key_grad, value_grad, output_grad, g...  208 us
    all_gather x1, waiting for transfers between devices, body(): lax.all_gather(up_weight, 'fsdp', axis=0, tiled=True)  162 us
    all_gather x1, waiting for transfers between devices, body(): lax.all_gather(down_weight, 'fsdp', axis=0, tiled=True)  154 us
    all_gather x1, waiting for transfers between devices, body(): lax.all_gather(gate_weight, 'fsdp', axis=0, tiled=True)  154 us
  transfers between devices with their start and end apart: 18, of which 13 were waited for; matrix products, arithmetic and copies ran while one was open for 5% of the time, Pallas kernels for 0%

profile of v1, /device:TPU:0, one launch (start us, length us, event | category | flops | bytes accessed | tf_op | source)
XLA Modules:
  0.0 2797.2 jit_solution(10149313225332794956)
XLA Ops:
  9.4 22.6 all-gather
  35.1 33.7 %all_gather.42 = bf16[2048,128]{1,0:T(8,128)(2,1)S(1)} all-gather(bf16[256,128]{1,0:T(8,128)(2,1)S(1)} %copy-done.47), channel_id=1, replica_groups=mesh['fsdp'=8,'ctx'=2,'tp'=2] {'fsdp'}, dimensions={0}, use_global_device_ids=true | all-gather | bytes 589824 | tf_op jit(solution)/shard_map/all_gather | solution.py:105
  75.1 32.7 %all_gather.40 = bf16[2048,128]{1,0:T(8,128)(2,1)S(1)} all-gather(bf16[256,128]{1,0:T(8,128)(2,1)S(1)} %copy-done.48), channel_id=1, replica_groups=mesh['fsdp'=8,'ctx'=2,'tp'=2] {'fsdp'}, dimensions={0}, use_global_device_ids=true | all-gather | bytes 589824 | tf_op jit(solution)/shard_map/all_gather | solution.py:106
  131.4 39.3 %all-gather.10.cloned.1.call-done = bf16[2048,1024]{1,0:T(8,128)(2,1)} async-done(((bf16[256,1024]{1,0:T(8,128)(2,1)}), bf16[2048,1024]{1,0:T(8,128)(2,1)}) %all-gather.10.cloned.1.call-update) | async-done | bytes 4194320 | tf_op jit(solution)/shard_map/all_gather | solution.py:160
  177.3 18.3 all-gather.1
  200.0 162.1 %all-gather.14.cloned.1.call-done = bf16[2048,2816]{1,0:T(8,128)(2,1)} async-done(((bf16[256,2816]{1,0:T(8,128)(2,1)}), bf16[2048,2816]{1,0:T(8,128)(2,1)}) %all-gather.14.cloned.1.call-update) | async-done | bytes 11534352 | tf_op jit(solution)/shard_map/all_gather | solution.py:170
  362.1 9.3 fusion.74
  371.4 154.2 %all-gather.12.cloned.1.call-done = bf16[2048,2816]{1,0:T(8,128)(2,1)} async-done(((bf16[256,2816]{1,0:T(8,128)(2,1)}), bf16[2048,2816]{1,0:T(8,128)(2,1)}) %all-gather.12.cloned.1.call-update) | async-done | bytes 11534352 | tf_op jit(solution)/shard_map/all_gather | solution.py:169
  525.6 9.3 fusion.73
  534.9 154.2 %all-gather.16.cloned.1.call-done = bf16[2048,2816]{1,0:T(8,128)(2,1)} async-done(((bf16[256,2816]{1,0:T(8,128)(2,1)}), bf16[2048,2816]{1,0:T(8,128)(2,1)}) %all-gather.16.cloned.1.call-update) | async-done | bytes 11534352 | tf_op jit(solution)/shard_map/all_gather | solution.py:186
  689.2 11.1 multiply_convert_fusion
  718.9 17.0 all-reduce.13.cloned.1.call-done
  777.8 11.6 reduce-scatter.10.cloned.1.call-done
  808.3 12.6 convolution_bitcast_fusion
  821.0 12.6 fusion.79
  833.9 12.6 fusion.78
  853.0 379.2 %all_to_all.5 = bf16[8,256,2816]{2,1,0:T(8,128)(2,1)S(1)} all-to-all(bf16[8,256,2816]{2,1,0:T(8,128)(2,1)} %stack.2), channel_id=1, replica_groups=mesh['fsdp'=8,'ctx'=2,'tp'=2] {'fsdp'}, dimensions={0} | all-to-all | bytes 23068672 | tf_op jit(solution)/shard_map/all_to_all | solution.py:179
  1243.3 118.2 %reduce-scatter.20.cloned.1.call-done = f32[256,1024]{1,0:T(8,128)} async-done(((f32[2048,1024]{1,0:T(8,128)}), f32[256,1024]{1,0:T(8,128)}) %reduce-scatter.20.cloned.1.call-update) | async-done | bytes 1048592 | tf_op jit(solution)/shard_map/reduce_scatter | solution.py:280
  1361.5 376.6 %reduce-scatter.26.cloned.1.call-done = f32[256,2816]{0,1:T(8,128)} async-done(((f32[2048,2816]{0,1:T(8,128)}), f32[256,2816]{0,1:T(8,128)}) %reduce-scatter.26.cloned.1.call-update) | async-done | bytes 2883600 | tf_op jit(solution)/shard_map/reduce_scatter | solution.py:280
  1738.1 375.8 %reduce-scatter.24.cloned.1.call-done = f32[256,2816]{1,0:T(8,128)} async-done(((f32[2048,2816]{1,0:T(8,128)}), f32[256,2816]{1,0:T(8,128)}) %reduce-scatter.24.cloned.1.call-update) | async-done | bytes 2883600 | tf_op jit(solution)/shard_map/reduce_scatter | solution.py:280
  2113.9 375.8 %reduce-scatter.22.cloned.1.call-done = f32[256,2816]{1,0:T(8,128)} async-done(((f32[2048,2816]{1,0:T(8,128)}), f32[256,2816]{1,0:T(8,128)}) %reduce-scatter.22.cloned.1.call-update) | async-done | bytes 2883600 | tf_op jit(solution)/shard_map/reduce_scatter | solution.py:280
  2491.6 28.6 %all-reduce.15.cloned.1.call-done = (f32[256,2048]{1,0:T(8,128)}, f32[256,2048]{1,0:T(8,128)}) async-done(((f32[256,2048]{1,0:T(8,128)}, f32[256,2048]{1,0:T(8,128)}), (f32[256,2048]{1,0:T(8,128)}, f32[256,2048]{1,0:T(8,128)})) %all-reduce.15.cloned.1.call-update) | async-done | bytes 4194320 | tf_op jit(solution)/shard_map/psum | solution.py:73
  2522.5 37.3 %all-reduce.2 = (f32[2048]{0:T(1024)S(1)}, f32[2048]{0:T(1024)S(1)}) all-reduce(f32[2048]{0:T(1024)S(1)} %get-tuple-element.46, f32[2048]{0:T(1024)S(1)} %copy-done.53), channel_id=4, replica_groups=mesh['fsdp'=8,'ctx'=2,'tp'=2] {'fsdp'}, use_global_device_ids=true, to_apply=%region_17.18.clone | all-reduce | flops 4096 | bytes 32768
  2570.8 208.2 %all-reduce.17.cloned.1.call-done = (f32[256,1024]{1,0:T(8,128)}, f32[256,128]{1,0:T(8,128)}, f32[256,128]{1,0:T(8,128)}, f32[256,1024]{1,0:T(8,128)}, f32[256,2...) async-done(((f32[256,1024]{1,0:T(8,128)}, f32[256,128]{1,0:T(8,128)}, f32[256,128]{1,0:T(8,128)}, f32[256,1024]{1,0:T(8,128)}, f32[256,2816]{1,0:T(8,128)}, ...) | async-done | bytes 11010064 | tf_op jit(solution)/shard_map/psum | solution.py:307
  (261 shorter events, 168.2 us)
Async XLA Ops:
  7.2 61.7 %copy-start.5 = (bf16[256,2048]{1,0:T(8,128)(2,1)S(1)}, bf16[256,2048]{1,0:T(8,128)(2,1)}, u32[]{:S(2)}) copy-start(bf16[256,2048]{1,0:T(8,128)(2,1)} %param.12) | copy-start | bytes 3145732
  7.2 106.9 %all-gather.8.cloned.1.call-start = ((), (), s32[]{:S(2)}) async-start(), calls=%async_computation.10 | async-start | bytes 4718592 | tf_op jit(solution)/shard_map/all_gather | solution.py:104
  7.9 162.7 %all-gather.10.cloned.1.call-start = ((), (), s32[]{:S(2)}) async-start(), calls=%async_computation.11 | async-start | bytes 4718592 | tf_op jit(solution)/shard_map/all_gather | solution.py:160
  8.7 187.0 %all-reduce.11.cloned.1.call-start = ((), (), s32[]{:S(2)}) async-start(), calls=%async_computation.12 | async-start | bytes 4194304 | tf_op jit(solution)/shard_map/psum | solution.py:73
  35.1 79.0 %copy-start.49 = (f32[256]{0:T(256)}, f32[256]{0:T(256)S(1)}, u32[]{:S(2)}) copy-start(f32[256]{0:T(256)S(1)} %get-tuple-element.83) | copy-start | bytes 3076
  130.5 40.2 %copy-start.38 = (bf16[64,8,256]{2,0,1:T(8,128)(2,1)}, bf16[64,8,256]{2,0,1:T(8,128)(2,1)S(1)}, u32[]{:S(2)}) copy-start(bf16[64,8,256]{2,0,1:T(8,128)(2,1)S(1)} %fusion.29) | copy-start | bytes 786436
  131.4 44.1 %copy-start.39 = (bf16[64,8,256]{2,0,1:T(8,128)(2,1)}, bf16[64,8,256]{2,0,1:T(8,128)(2,1)S(1)}, u32[]{:S(2)}) copy-start(bf16[64,8,256]{2,0,1:T(8,128)(2,1)S(1)} %fusion.30) | copy-start | bytes 786436
  175.5 186.5 %all-gather.14.cloned.1.call-start = ((), (), s32[]{:S(2)}) async-start(), calls=%async_computation.14 | async-start | bytes 12976128 | tf_op jit(solution)/shard_map/all_gather | solution.py:170
  176.1 349.5 %all-gather.12.cloned.1.call-start = ((), (), s32[]{:S(2)}) async-start(), calls=%async_computation.13 | async-start | bytes 12976128 | tf_op jit(solution)/shard_map/all_gather | solution.py:169
  176.7 512.5 %all-gather.16.cloned.1.call-start = ((), (), s32[]{:S(2)}) async-start(), calls=%async_computation.15 | async-start | bytes 12976128 | tf_op jit(solution)/shard_map/all_gather | solution.py:186
  177.3 558.6 %all-reduce.13.cloned.1.call-start = ((), (), s32[]{:S(2)}) async-start(), calls=%async_computation.16 | async-start | bytes 4194304 | tf_op jit(solution)/shard_map/psum | solution.py:73
  716.2 58.6 %reduce-scatter.12.cloned.1.call-start = ((), (), s32[]{:S(2)}) async-start(), calls=%async_computation.18 | async-start | bytes 393216 | tf_op jit(solution)/shard_map/reduce_scatter | solution.py:247
  761.7 27.7 reduce-scatter.10.cloned.1.call-start
  771.7 471.6 %reduce-scatter.18.cloned.1.call-start = ((), (), s32[]{:S(2)}) async-start(), calls=%async_computation.21 | async-start | bytes 1179648 | tf_op jit(solution)/shard_map/reduce_scatter | solution.py:280
  777.3 466.0 %reduce-scatter.16.cloned.1.call-start = ((), (), s32[]{:S(2)}) async-start(), calls=%async_computation.20 | async-start | bytes 1179648 | tf_op jit(solution)/shard_map/reduce_scatter | solution.py:280
  792.9 450.4 %reduce-scatter.14.cloned.1.call-start = ((), (), s32[]{:S(2)}) async-start(), calls=%async_computation.19 | async-start | bytes 9437184 | tf_op jit(solution)/shard_map/reduce_scatter | solution.py:280
  801.8 559.7 %reduce-scatter.20.cloned.1.call-start = ((), (), s32[]{:S(2)}) async-start(), calls=%async_computation.22 | async-start | bytes 9437184 | tf_op jit(solution)/shard_map/reduce_scatter | solution.py:280
  808.2 929.9 %reduce-scatter.26.cloned.1.call-start = ((), (), s32[]{:S(2)}) async-start(), calls=%async_computation.25 | async-start | bytes 25952256 | tf_op jit(solution)/shard_map/reduce_scatter | solution.py:280
  820.9 1293.0 %reduce-scatter.24.cloned.1.call-start = ((), (), s32[]{:S(2)}) async-start(), calls=%async_computation.24 | async-start | bytes 25952256 | tf_op jit(solution)/shard_map/reduce_scatter | solution.py:280
  833.6 1656.1 %reduce-scatter.22.cloned.1.call-start = ((), (), s32[]{:S(2)}) async-start(), calls=%async_computation.23 | async-start | bytes 25952256 | tf_op jit(solution)/shard_map/reduce_scatter | solution.py:280
  846.5 1673.7 %all-reduce.15.cloned.1.call-start = ((), (), s32[]{:S(2)}) async-start(), calls=%async_computation.26 | async-start | bytes 8388608 | tf_op jit(solution)/shard_map/psum | solution.py:73
  853.0 379.2 %copy-start.15 = (bf16[256,2816]{1,0:T(8,128)(2,1)S(1)}, bf16[256,2816]{1,0:T(8,128)(2,1)}, u32[]{:S(2)}) copy-start(bf16[256,2816]{1,0:T(8,128)(2,1)} %get-tuple-element.65) | copy-start | bytes 4325380
  1243.2 1535.8 %all-reduce.17.cloned.1.call-start = ((), (), s32[]{:S(2)}) async-start(), calls=%async_computation.27 | async-start | bytes 22020096 | tf_op jit(solution)/shard_map/psum | solution.py:307
  2489.8 75.9 %copy-start.57 = (f32[256]{0:T(256)S(1)}, f32[256]{0:T(256)}, u32[]{:S(2)}) copy-start(f32[256]{0:T(256)} %get-tuple-element.82) | copy-start | bytes 3076
  (56 other events, 218.0 us)
Sparse Core Ops, SparseCore 0:
  10.1 86.2 all-gather.7
  98.6 72.0 all-gather.9
  175.6 19.8 all-reduce.10
  197.5 164.4 all-gather.13
  364.1 161.4 all-gather.11
  527.7 161.4 all-gather.15
  716.3 19.4 all-reduce.12
  761.8 12.9 reduce-scatter.11
  777.6 11.7 reduce-scatter.9
  793.2 64.1 reduce-scatter.17
  861.4 74.2 reduce-scatter.15
  939.2 268.8 reduce-scatter.13
  1211.7 149.8 reduce-scatter.19
  1365.3 372.7 reduce-scatter.25
  1741.8 372.0 reduce-scatter.23
  2117.6 372.0 reduce-scatter.21
  2492.7 27.5 all-reduce.14
  2523.1 255.8 all-reduce.16
